TPU v7x, 512 devices: a whole 4x4x16 slice. The times are simulated.
512 devices in a mesh: cond: 2 (over core), kern: 8 (over y, x_hi), tile: 32 (over x_lo, z).
Axes of the slice: x: 4 (x_hi: 2, x_lo: 2; x = x_hi * 2 + x_lo), y: 4, z: 16, core: 2. Of those that a mesh axis runs over, the one named last changes fastest.
Arguments:
- mask: bfloat16 [1, 1024, 1024], P(None, 'tile'), may hold values from -6 to 6
- kernels: bfloat16 [2, 4, 24, 512, 512], P(None, 'cond', 'kern', 'tile'), may hold values from -6 to 6
- kernel_weights: float32 [4, 24], P('cond', 'kern'), may hold values from 0.02 to 0.2
Outputs:
- low: float32 [1, 1024, 1024], P(None, 'tile', 'kern')
- high: float32 [1, 1024, 1024], P(None, 'tile', 'kern')
All inputs are finite; a program needn't handle non-finite values.
Results may differ from a plain program's by a relative error of at most 0.0032.
Values may be sent and summed in bfloat16 or wider, within the bound.
No kernel may reach another device: no remote copies, remote signals or barrier semaphores. Data moves between devices by JAX's collectives and lax.ppermute only.
A program may use at most 64 MiB of HBM per device.

v0:
```python
import math

import jax
import jax.numpy as jnp
import numpy as np
from jax import lax
from jax.experimental import pallas as pl
from jax.experimental.pallas import tpu as pltpu
from jax.sharding import PartitionSpec as P

BF = jnp.bfloat16
F32 = jnp.float32
TN = (((0,), (0,)), ((), ()))
NN = (((1,), (0,)), ((), ()))
NT = (((1,), (1,)), ((), ()))


def tables(length, count):
    pixel = np.arange(length, dtype=np.int64)[:, None]
    freq = np.arange(count, dtype=np.int64)[None, :] - count // 2
    phase = np.mod(pixel * freq, length).astype(np.float32) * np.float32(2.0 * math.pi / length)
    factor = np.float32(1.0 / math.sqrt(length))
    return (
        (np.cos(phase) * factor).astype(BF),
        (np.sin(phase) * factor).astype(BF),
    )


def dot(a, b, dims):
    return lax.dot_general(a, b, dims, preferred_element_type=F32)


def regroup(blocks, lanes):
    group = (lax.broadcasted_iota(jnp.int32, blocks[0].shape, 1) // 32) % 4
    outs = []
    for b in range(4):
        moved = [
            blk if q == b else pltpu.roll(blk, (32 * (q - b)) % lanes, 1)
            for q, blk in enumerate(blocks)
        ]
        low = jnp.where(group == 0, moved[0], moved[1])
        high = jnp.where(group == 2, moved[2], moved[3])
        outs.append(jnp.where(group < 2, low, high))
    return outs


def rows_kernel(mask_ref, table_ref, sign_ref, out_ref):
    rows, pixels = mask_ref.shape
    half = pixels // 2
    both = jnp.concatenate([mask_ref[:, :half], mask_ref[:, half:]], axis=0)
    part = dot(both, table_ref[...], NN)
    out = part[:rows] + part[rows:] * sign_ref[...]
    width = out.shape[1] // 4
    stacked = jnp.concatenate([out[:, g * width : (g + 1) * width] for g in range(4)], axis=0)
    out_ref[...] = stacked.T.astype(BF)


def half_kernel(cols_ref, kern_ref, table_ref, out_ref):
    tiles = cols_ref.shape[0] // 8
    count = kern_ref.shape[3]
    cols = cols_ref[...].astype(F32).reshape(tiles // 4, 4, 8, 128)
    blocks = [
        jnp.concatenate([cols[D, b] for D in range(tiles // 4)], axis=1) for b in range(4)
    ]
    groups = regroup(blocks, 32 * tiles)
    lines = jnp.concatenate(groups, axis=0).astype(BF)
    part = dot(lines, table_ref[...], NN)
    spec_re = part[:16, :count] + part[16:, count:]
    spec_im = part[16:, :count] - part[:16, count:]
    top, low = [], []
    items = kern_ref.shape[1]
    for n in range(items):
        kre = kern_ref[0, n].astype(F32)
        kim = kern_ref[1, n].astype(F32)
        fre = (spec_re * kre - spec_im * kim).astype(BF)
        fim = (spec_re * kim + spec_im * kre).astype(BF)
        top.append(jnp.concatenate([fre, -fim], axis=1))
        low.append(jnp.concatenate([fim, fre], axis=1))
    lhs = jnp.concatenate(top + low, axis=0)
    fields = dot(lhs, table_ref[...], NT)
    pick = lambda ri, n: fields[(ri * items + n) * 16 : (ri * items + n + 1) * 16]
    quads = (
        [pick(0, n) for n in range(4)],
        [pick(1, n) for n in range(4)],
        [pick(0, 4), pick(0, 5), pick(1, 4), pick(1, 5)],
    )
    for at, quad in enumerate(quads):
        for b, moved in enumerate(regroup(quad, 32 * tiles)):
            moved = moved.astype(BF)
            for D in range(tiles // 4):
                out_ref[4 * D + b, 16 * at : 16 * at + 16] = moved[:, 128 * D : 128 * D + 128]


def power_kernel(half_ref, weight_ref, table_ref, out_ref):
    tiles = half_ref.shape[0]
    conds, kerns = weight_ref.shape
    quad = [half_ref[:, 16 * q : 16 * q + 16, :].reshape(16 * tiles, 128).T for q in range(3)]
    half_re = jnp.concatenate([quad[0], quad[2][:64]], axis=0)
    half_im = jnp.concatenate([quad[1], quad[2][64:]], axis=0)
    field_re = dot(jnp.concatenate([half_re, -half_im], axis=1), table_ref[...], NT)
    field_im = dot(jnp.concatenate([half_im, half_re], axis=1), table_ref[...], NT)
    power = field_re * field_re + field_im * field_im
    for c in range(conds):
        total = None
        for k in range(kerns):
            n = c * kerns + k
            term = power[32 * n : 32 * n + 32] * weight_ref[c, k]
            total = term if total is None else total + term
        for d in range(out_ref.shape[0]):
            out_ref[d, 32 * c : 32 * c + 32] = total[:, 128 * d : 128 * d + 128]


def bounds_kernel(parts_ref, out_ref):
    total = parts_ref[0]
    for s in range(1, parts_ref.shape[0]):
        total = total + parts_ref[s]
    out_ref[:32] = jnp.minimum(total[:32], total[32:])
    out_ref[32:] = jnp.maximum(total[:32], total[32:])


def call(body, shape, dtype, *args, smem=()):
    return pl.pallas_call(
        body,
        out_shape=jax.ShapeDtypeStruct(shape, dtype),
        in_specs=[
            pl.BlockSpec(memory_space=pltpu.SMEM if n in smem else pltpu.VMEM)
            for n in range(len(args))
        ],
        out_specs=pl.BlockSpec(memory_space=pltpu.VMEM),
        compiler_params=pltpu.CompilerParams(vmem_limit_bytes=48 * 1024 * 1024),
        name=body.__name__,
    )(*args)


def local(mask, kernels, kernel_weights):
    _, rows, pixels = mask.shape
    conds, kerns = kernel_weights.shape
    count = kernels.shape[4]
    tiles, groups = lax.axis_size("tile"), lax.axis_size("kern")
    cos_table, sin_table = tables(pixels, count)
    table = jnp.asarray(np.concatenate([cos_table, sin_table], axis=1))
    order = np.arange(count).reshape(tiles, 2, 8).transpose(1, 0, 2).reshape(-1)
    row_table = np.concatenate([cos_table[:, order], -sin_table[:, order]], axis=1)
    sign = np.where((order - count // 2) % 2 == 0, 1.0, -1.0).astype(np.float32)
    row_table = jnp.asarray(row_table[: pixels // 2])
    sign = jnp.asarray(np.concatenate([sign, sign])[None])

    sent = call(rows_kernel, (8 * tiles, 128), BF, mask[0], row_table, sign)
    cols = lax.all_to_all(sent, "tile", split_axis=0, concat_axis=0, tiled=True)
    kern = kernels.reshape(2, conds * kerns, kernels.shape[3], count)
    half = call(half_kernel, (tiles, 48, 128), BF, cols, kern, table)
    half = lax.all_to_all(half, "tile", split_axis=0, concat_axis=0, tiled=True)
    weighted = call(power_kernel, (groups, 64, 128), F32, half, kernel_weights, table, smem=(1,))
    parts = lax.all_to_all(weighted, "kern", split_axis=0, concat_axis=0, tiled=True)
    band = call(bounds_kernel, (64, 128), F32, parts)
    bands = lax.all_gather(band, "cond")
    low = jnp.minimum(bands[0, :32], bands[1, :32])
    high = jnp.maximum(bands[0, 32:], bands[1, 32:])
    return (low[None], high[None])


def solution(mesh):
    placed = (P(None, "tile", None), P(None, "cond", "kern", "tile", None), P("cond", "kern"))
    return jax.shard_map(
        local,
        mesh=mesh,
        in_specs=placed,
        out_specs=(P(None, "tile", "kern"), P(None, "tile", "kern")),
        check_vma=False,
    )
```

profile of v0, /device:TPU:1, one launch (start us, length us, event | category | flops | bytes accessed | tf_op | source)
XLA Modules:
  0.0 88.9 jit_solution(8901359499192893354)
XLA Ops:
  0.6 0.0 copy-start.2
  0.6 1.2 %copy-done.2 = bf16[512,1024]{1,0:T(8,128)(2,1)S(1)} copy-done((bf16[512,1024]{1,0:T(8,128)(2,1)S(1)}, bf16[512,1024]{1,0:T(8,128)(2,1)}, u32[]{:S(2)}) %copy-start.2) | copy-done | bytes 1048600
  1.9 0.0 copy-start.4
  1.9 0.8 copy-done.4
  2.7 0.0 copy-start.5
  2.7 0.7 copy-done.5
  3.4 0.4 rows_kernel.1
  3.8 0.0 copy-start.6
  3.8 30.0 %all_to_all.21 = bf16[32,8,128]{2,1,0:T(8,128)(2,1)S(1)} all-to-all(bf16[32,8,128]{2,1,0:T(8,128)(2,1)S(1)} %bitcast.5), channel_id=1, replica_groups=mesh['cond'=2,'kern'=8,'tile'=32] {'tile'}, dimensions={0} | all-to-all | bytes 131072 | tf_op jit(solution)/shard_map/all_to_all | solution.py:149
  33.7 0.0 copy-start
  33.7 1.6 %copy-done = bf16[1024,1024]{1,0:T(8,128)(2,1)S(1)} copy-done((bf16[1024,1024]{1,0:T(8,128)(2,1)S(1)}, bf16[1024,1024]{1,0:T(8,128)(2,1)}, u32[]{:S(2)}) %copy-start) | copy-done | bytes 2097176
  35.3 0.0 copy-start.3
  35.3 0.9 %copy-done.3 = bf16[2,2,3,16,512]{4,3,2,1,0:T(8,128)(2,1)S(1)} copy-done((bf16[2,2,3,16,512]{4,3,2,1,0:T(8,128)(2,1)S(1)}, bf16[2,2,3,16,512]{4,3,2,1,0:T(8,128)(2,1)}, u32[]{:S(2)}) %copy-start.3) | copy-done | bytes 196632
  36.3 0.0 copy-start.1
  36.3 1.5 %half_kernel.1 = bf16[32,48,128]{2,1,0:T(8,128)(2,1)S(1)} custom-call(bf16[256,128]{1,0:T(8,128)(2,1)S(1)} %bitcast.6, bf16[2,6,16,512]{3,2,1,0:T(8,128)(2,1)S(1)} %bitcast.7, bf16[1024,1024]{1,0:T(8,128)(2,1)S(1)} %copy-done), custom_call_target="tpu_custom_call" | custom-call | tf_op jit(solution)/shard_map/half_kernel/pallas_call | solution.py:122
  37.8 26.7 %all_to_all.22.half_ref = bf16[32,48,128]{2,1,0:T(8,128)(2,1)S(1)} all-to-all(bf16[32,48,128]{2,1,0:T(8,128)(2,1)S(1)} %half_kernel.1), channel_id=1, replica_groups=mesh['cond'=2,'kern'=8,'tile'=32] {'tile'}, dimensions={0} | all-to-all | bytes 786432 | tf_op jit(solution)/shard_map/all_to_all | solution.py:152
  64.5 0.0 copy-done.6
  64.5 0.0 copy-done.1
  64.5 2.1 %power_kernel.1 = f32[8,64,128]{2,1,0:T(8,128)S(1)} custom-call(bf16[32,48,128]{2,1,0:T(8,128)(2,1)S(1)} %all_to_all.22.half_ref, f32[2,3]{1,0:T(2,128)S(1)} %copy-done.6, bf16[1024,1024]{1,0:T(8,128)(2,1)S(1)} %copy-done.1), custom_call_target="tpu_custom_call" | custom-call | tf_op jit(solution)/shard_map/power_kernel/pallas_call | solution.py:122
  66.6 13.8 %all_to_all.23.parts_ref = f32[8,64,128]{2,1,0:T(8,128)S(1)} all-to-all(f32[8,64,128]{2,1,0:T(8,128)S(1)} %power_kernel.1), channel_id=1, replica_groups=mesh['cond'=2,'kern'=8,'tile'=32] {'kern'}, dimensions={0} | all-to-all | bytes 524288 | tf_op jit(solution)/shard_map/all_to_all | solution.py:154
  80.4 7.8 %all-gather = f32[128,128]{1,0:T(8,128)S(1)} all-gather(f32[64,128]{1,0:T(8,128)S(1)} %bounds_kernel.1), channel_id=2, replica_groups=mesh['cond'=2,'kern'=8,'tile'=32] {'cond'}, dimensions={0}, use_global_device_ids=true | all-gather | bytes 98304 | tf_op jit(solution)/shard_map/all_gather | solution.py:156
  88.2 0.6 slice_maximum_fusion
  (1 shorter events, 0.0 us)
Async XLA Ops:
  0.6 1.2 %copy-start.2 = (bf16[512,1024]{1,0:T(8,128)(2,1)S(1)}, bf16[512,1024]{1,0:T(8,128)(2,1)}, u32[]{:S(2)}) copy-start(bf16[512,1024]{1,0:T(8,128)(2,1)} %constant.7.clone.table_ref) | copy-start | bytes 3145732
  1.9 0.8 copy-start.4
  2.7 0.7 copy-start.5
  3.8 60.7 %copy-start.6 = (f32[2,3]{1,0:T(2,128)S(1)}, f32[2,3]{1,0:T(2,128)}, u32[]{:S(2)}) copy-start(f32[2,3]{1,0:T(2,128)} %weight_ref.1) | copy-start | bytes 76
  33.7 1.6 %copy-start = (bf16[1024,1024]{1,0:T(8,128)(2,1)S(1)}, bf16[1024,1024]{1,0:T(8,128)(2,1)}, u32[]{:S(2)}) copy-start(bf16[1024,1024]{1,0:T(8,128)(2,1)} %constant.6.clone.table_ref) | copy-start | bytes 6291460
  35.3 0.9 %copy-start.3 = (bf16[2,2,3,16,512]{4,3,2,1,0:T(8,128)(2,1)S(1)}, bf16[2,2,3,16,512]{4,3,2,1,0:T(8,128)(2,1)}, u32[]{:S(2)}) copy-start(bf16[2,2,3,16,512]{4,3,2,1,0:T(8,128)(2,1)} %param.7) | copy-start | bytes 589828
  36.3 28.2 %copy-start.1 = (bf16[1024,1024]{1,0:T(8,128)(2,1)S(1)}, bf16[1024,1024]{1,0:T(8,128)(2,1)}, u32[]{:S(2)}) copy-start(bf16[1024,1024]{1,0:T(8,128)(2,1)} %constant.6.clone.table_ref) | copy-start | bytes 6291460
where the time goes:
time: 89.2 us; the launch traced here: 88.9 us
  blocking collectives  78.3 us (88%)
  local copies, waits for them, and re-layouts  5.27 us (6%)
  Pallas kernels  4.02 us (5%)
    all_to_all x1, blocking collectives, local(): cols = lax.all_to_all(sent, 'tile', split_axis=0, concat_axis=0, tiled=True)  30 us
    all_to_all x1, blocking collectives, local(): half = lax.all_to_all(half, 'tile', split_axis=0, concat_axis=0, tiled=True)  26.7 us
    all_to_all x1, blocking collectives, local(): lax.all_to_all(weighted, 'kern', split_axis=0, concat_axis=0, tiled=True)  13.8 us
    all_gather x1, blocking collectives, local(): bands = lax.all_gather(band, 'cond')  7.83 us
    unnamed x14, local copies, waits for them, and re-layouts  5.27 us
    pallas_call x4, Pallas kernels, call(): pl.pallas_call(body, out_shape=jax.ShapeDtypeStruct(shape, dtype), in_spe...  4.02 us

commit v1 on v0

--- a/solution.py
+++ b/solution.py
@@ -44,15 +44,26 @@
     return outs
 
 
-def rows_kernel(mask_ref, table_ref, sign_ref, out_ref):
-    rows, pixels = mask_ref.shape
+def rows_kernel(
+    mask_ref, rows_ref, table_ref, kern_ref, out_ref, table_out, kern_out, mask_buf, table_buf, sems
+):
+    pairs = [(mask_ref, mask_buf), (rows_ref, table_buf), (table_ref, table_out), (kern_ref, kern_out)]
+    copies = [pltpu.make_async_copy(src, dst, sems.at[n]) for n, (src, dst) in enumerate(pairs)]
+    for copy in copies:
+        copy.start()
+    for copy in copies[:2]:
+        copy.wait()
+    rows, pixels = mask_buf.shape
     half = pixels // 2
-    both = jnp.concatenate([mask_ref[:, :half], mask_ref[:, half:]], axis=0)
-    part = dot(both, table_ref[...], NN)
-    out = part[:rows] + part[rows:] * sign_ref[...]
+    both = jnp.concatenate([mask_buf[:, :half], mask_buf[:, half:]], axis=0)
+    part = dot(both, table_buf[...], NN)
+    odd = lax.broadcasted_iota(jnp.int32, (rows, part.shape[1]), 1) % 2 == 1
+    out = part[:rows] + jnp.where(odd, -part[rows:], part[rows:])
     width = out.shape[1] // 4
     stacked = jnp.concatenate([out[:, g * width : (g + 1) * width] for g in range(4)], axis=0)
     out_ref[...] = stacked.T.astype(BF)
+    for copy in copies[2:]:
+        copy.wait()
 
 
 def half_kernel(cols_ref, kern_ref, table_ref, out_ref):
@@ -106,27 +117,34 @@
             n = c * kerns + k
             term = power[32 * n : 32 * n + 32] * weight_ref[c, k]
             total = term if total is None else total + term
+        total = total.astype(BF)
         for d in range(out_ref.shape[0]):
-            out_ref[d, 32 * c : 32 * c + 32] = total[:, 128 * d : 128 * d + 128]
+            at = d % (total.shape[1] // 128) * 128
+            out_ref[d, 32 * c : 32 * c + 32] = total[:, at : at + 128]
 
 
-def bounds_kernel(parts_ref, out_ref):
-    total = parts_ref[0]
-    for s in range(1, parts_ref.shape[0]):
-        total = total + parts_ref[s]
-    out_ref[:32] = jnp.minimum(total[:32], total[32:])
-    out_ref[32:] = jnp.maximum(total[:32], total[32:])
+def bounds_kernel(parts_ref, low_ref, high_ref):
+    halves = []
+    kern = parts_ref.shape[0] // 2
+    for group in range(2):
+        total = parts_ref[group * kern].astype(F32)
+        for s in range(1, kern):
+            total = total + parts_ref[group * kern + s].astype(F32)
+        halves += [total[:32], total[32:]]
+    low_ref[...] = jnp.minimum(jnp.minimum(halves[0], halves[1]), jnp.minimum(halves[2], halves[3]))
+    high_ref[...] = jnp.maximum(jnp.maximum(halves[0], halves[1]), jnp.maximum(halves[2], halves[3]))
 
 
-def call(body, shape, dtype, *args, smem=()):
+def call(body, shapes, *args, spaces={}, scratch=(), cost=None):
     return pl.pallas_call(
         body,
-        out_shape=jax.ShapeDtypeStruct(shape, dtype),
+        out_shape=shapes,
         in_specs=[
-            pl.BlockSpec(memory_space=pltpu.SMEM if n in smem else pltpu.VMEM)
-            for n in range(len(args))
+            pl.BlockSpec(memory_space=spaces.get(n, pltpu.VMEM)) for n in range(len(args))
         ],
-        out_specs=pl.BlockSpec(memory_space=pltpu.VMEM),
+        out_specs=jax.tree.map(lambda _: pl.BlockSpec(memory_space=pltpu.VMEM), shapes),
+        scratch_shapes=scratch,
+        cost_estimate=cost,
         compiler_params=pltpu.CompilerParams(vmem_limit_bytes=48 * 1024 * 1024),
         name=body.__name__,
     )(*args)
@@ -136,26 +154,34 @@
     _, rows, pixels = mask.shape
     conds, kerns = kernel_weights.shape
     count = kernels.shape[4]
-    tiles, groups = lax.axis_size("tile"), lax.axis_size("kern")
+    tiles, groups = lax.axis_size("tile"), lax.axis_size("kern") * lax.axis_size("cond")
     cos_table, sin_table = tables(pixels, count)
     table = jnp.asarray(np.concatenate([cos_table, sin_table], axis=1))
     order = np.arange(count).reshape(tiles, 2, 8).transpose(1, 0, 2).reshape(-1)
     row_table = np.concatenate([cos_table[:, order], -sin_table[:, order]], axis=1)
-    sign = np.where((order - count // 2) % 2 == 0, 1.0, -1.0).astype(np.float32)
     row_table = jnp.asarray(row_table[: pixels // 2])
-    sign = jnp.asarray(np.concatenate([sign, sign])[None])
+    shape = jax.ShapeDtypeStruct
 
-    sent = call(rows_kernel, (8 * tiles, 128), BF, mask[0], row_table, sign)
+    kern = kernels.reshape(2, conds * kerns, kernels.shape[3], count)
+    sent, table, kern = call(
+        rows_kernel,
+        (shape((8 * tiles, 128), BF), shape(table.shape, BF), shape(kern.shape, BF)),
+        *(pltpu.with_memory_space_constraint(a, pltpu.HBM) for a in (mask[0], row_table, table, kern)),
+        spaces={n: pltpu.HBM for n in range(4)},
+        scratch=[
+            pltpu.VMEM((rows, pixels), BF),
+            pltpu.VMEM(row_table.shape, BF),
+            pltpu.SemaphoreType.DMA((4,)),
+        ],
+    )
     cols = lax.all_to_all(sent, "tile", split_axis=0, concat_axis=0, tiled=True)
-    kern = kernels.reshape(2, conds * kerns, kernels.shape[3], count)
-    half = call(half_kernel, (tiles, 48, 128), BF, cols, kern, table)
+    half = call(half_kernel, shape((tiles, 48, 128), BF), cols, kern, table)
     half = lax.all_to_all(half, "tile", split_axis=0, concat_axis=0, tiled=True)
-    weighted = call(power_kernel, (groups, 64, 128), F32, half, kernel_weights, table, smem=(1,))
-    parts = lax.all_to_all(weighted, "kern", split_axis=0, concat_axis=0, tiled=True)
-    band = call(bounds_kernel, (64, 128), F32, parts)
-    bands = lax.all_gather(band, "cond")
-    low = jnp.minimum(bands[0, :32], bands[1, :32])
-    high = jnp.maximum(bands[0, 32:], bands[1, 32:])
+    weighted = call(
+        power_kernel, shape((groups, 64, 128), BF), half, kernel_weights, table, spaces={1: pltpu.SMEM}
+    )
+    parts = lax.all_to_all(weighted, ("cond", "kern"), split_axis=0, concat_axis=0, tiled=True)
+    low, high = call(bounds_kernel, (shape((32, 128), F32),) * 2, parts)
     return (low[None], high[None])
 
 

time: 89.2 us -> 83.2 us (0.933)
  local copies, waits for them, and re-layouts: 5.27 us -> 0.01 us
  Pallas kernels: 4.02 us -> 6.28 us
  blocking collectives: 78.3 us -> 76.1 us
    all_gather x1 -> x0, blocking collectives: 7.83 us -> none  [local(): bands = lax.all_gather(band, 'cond')]
    all_to_all x1, blocking collectives: 13.8 us -> 19.4 us  [local(): lax.all_to_all(weighted, ('cond', 'kern'), split_axis=0, concat_axis=0, t...]
    unnamed x14 -> x2, local copies, waits for them, and re-layouts: 5.27 us -> 0.01 us
    pallas_call x4, Pallas kernels: 4.02 us -> 6.28 us  [call(): pl.pallas_call(body, out_shape=shapes, in_specs=[pl.BlockSpec(memory_spac...]
where the time goes in v1:
time: 83.2 us; the launch traced here: 83 us
  blocking collectives  76.1 us (91%)
  Pallas kernels  6.28 us (8%)
    all_to_all x1, blocking collectives, local(): cols = lax.all_to_all(sent, 'tile', split_axis=0, concat_axis=0, tiled=True)  30 us
    all_to_all x1, blocking collectives, local(): half = lax.all_to_all(half, 'tile', split_axis=0, concat_axis=0, tiled=True)  26.7 us
    all_to_all x1, blocking collectives, local(): lax.all_to_all(weighted, ('cond', 'kern'), split_axis=0, concat_axis=0, t...  19.4 us
    pallas_call x4, Pallas kernels, call(): pl.pallas_call(body, out_shape=shapes, in_specs=[pl.BlockSpec(memory_spac...  6.28 us

profile of v1, /device:TPU:1, one launch (start us, length us, event | category | flops | bytes accessed | tf_op | source)
XLA Modules:
  0.0 83.0 jit_solution(14188009062545476932)
XLA Ops:
  0.6 2.0 %rows_kernel.1 = (bf16[256,128]{1,0:T(8,128)(2,1)S(1)}, bf16[1024,1024]{1,0:T(8,128)(2,1)S(1)}, bf16[2,6,16,512]{3,2,1,0:T(8,128)(2,1)S(1)}) custom-call(bf16[32,1024]{1,0:T(8,128)(2,1)} %bitcast.9, bf16[512,1024]{1,0:T(8,128)(2,1)} %constant.5.clone.rows_ref, bf16[1024,1024]{1,0:T(8,128)(2,1)} %constant.4.clone.table_ref, bf16[2,6,16,512]{3,2,1,0:T(8,128)(2,1)} %bitcast.8), custom_call_target="tpu_custom_call" | custom-call | tf_op jit(solution)/shard_map/rows_kernel/pallas_call | solution.py:139
  2.6 0.0 copy-start
  2.6 30.0 %all_to_all.21 = bf16[32,8,128]{2,1,0:T(8,128)(2,1)S(1)} all-to-all(bf16[32,8,128]{2,1,0:T(8,128)(2,1)S(1)} %bitcast.7), channel_id=1, replica_groups=mesh['cond'=2,'kern'=8,'tile'=32] {'tile'}, dimensions={0} | all-to-all | bytes 131072 | tf_op jit(solution)/shard_map/all_to_all | solution.py:177
  32.6 1.5 %half_kernel.1 = bf16[32,48,128]{2,1,0:T(8,128)(2,1)S(1)} custom-call(bf16[256,128]{1,0:T(8,128)(2,1)S(1)} %bitcast.6, bf16[2,6,16,512]{3,2,1,0:T(8,128)(2,1)S(1)} %get-tuple-element.8.kern_ref, bf16[1024,1024]{1,0:T(8,128)(2,1)S(1)} %get-tuple-element.9.table_ref), custom_call_target="tpu_custom_call" | custom-call | tf_op jit(solution)/shard_map/half_kernel/pallas_call | solution.py:139
  34.2 26.7 %all_to_all.22.half_ref = bf16[32,48,128]{2,1,0:T(8,128)(2,1)S(1)} all-to-all(bf16[32,48,128]{2,1,0:T(8,128)(2,1)S(1)} %half_kernel.1), channel_id=1, replica_groups=mesh['cond'=2,'kern'=8,'tile'=32] {'tile'}, dimensions={0} | all-to-all | bytes 786432 | tf_op jit(solution)/shard_map/all_to_all | solution.py:179
  60.8 0.0 copy-done
  60.8 2.1 %power_kernel.1 = bf16[16,64,128]{2,1,0:T(8,128)(2,1)S(1)} custom-call(bf16[32,48,128]{2,1,0:T(8,128)(2,1)S(1)} %all_to_all.22.half_ref, f32[2,3]{1,0:T(2,128)S(1)} %copy-done, bf16[1024,1024]{1,0:T(8,128)(2,1)S(1)} %get-tuple-element.9.table_ref), custom_call_target="tpu_custom_call" | custom-call | tf_op jit(solution)/shard_map/power_kernel/pallas_call | solution.py:139
  62.9 19.4 %all_to_all.23.parts_ref = bf16[16,64,128]{2,1,0:T(8,128)(2,1)S(1)} all-to-all(bf16[16,64,128]{2,1,0:T(8,128)(2,1)S(1)} %power_kernel.1), channel_id=1, replica_groups=mesh['cond'=2,'kern'=8,'tile'=32] {'cond','kern'}, dimensions={0} | all-to-all | bytes 524288 | tf_op jit(solution)/shard_map/all_to_all | solution.py:183
  82.4 0.7 bounds_kernel.1
Async XLA Ops:
  2.6 58.2 %copy-start = (f32[2,3]{1,0:T(2,128)S(1)}, f32[2,3]{1,0:T(2,128)}, u32[]{:S(2)}) copy-start(f32[2,3]{1,0:T(2,128)} %weight_ref.1) | copy-start | bytes 76

commit v2 on v1

--- a/solution.py
+++ b/solution.py
@@ -1,3 +1,4 @@
+import functools
 import math
 
 import jax
@@ -13,6 +14,10 @@
 TN = (((0,), (0,)), ((), ()))
 NN = (((1,), (0,)), ((), ()))
 NT = (((1,), (1,)), ((), ()))
+
+
+def rotated(count, first):
+    return [(first + at) % count for at in range(count)]
 
 
 def tables(length, count):
@@ -66,16 +71,16 @@
         copy.wait()
 
 
-def half_kernel(cols_ref, kern_ref, table_ref, out_ref):
+def half_kernel(cols_ref, kern_ref, table_ref, out_ref, *, came, goes):
     tiles = cols_ref.shape[0] // 8
     count = kern_ref.shape[3]
-    cols = cols_ref[...].astype(F32).reshape(tiles // 4, 4, 8, 128)
+    cols = cols_ref[...].astype(F32).reshape(tiles, 8, 128)
     blocks = [
-        jnp.concatenate([cols[D, b] for D in range(tiles // 4)], axis=1) for b in range(4)
+        jnp.concatenate([cols[came[4 * D + b]] for D in range(tiles // 4)], axis=1) for b in range(4)
     ]
     groups = regroup(blocks, 32 * tiles)
     lines = jnp.concatenate(groups, axis=0).astype(BF)
-    part = dot(lines, table_ref[...], NN)
+    part = dot(lines, table_ref[...], NT)
     spec_re = part[:16, :count] + part[16:, count:]
     spec_im = part[16:, :count] - part[:16, count:]
     top, low = [], []
@@ -88,7 +93,7 @@
         top.append(jnp.concatenate([fre, -fim], axis=1))
         low.append(jnp.concatenate([fim, fre], axis=1))
     lhs = jnp.concatenate(top + low, axis=0)
-    fields = dot(lhs, table_ref[...], NT)
+    fields = dot(lhs, table_ref[...], NN)
     pick = lambda ri, n: fields[(ri * items + n) * 16 : (ri * items + n + 1) * 16]
     quads = (
         [pick(0, n) for n in range(4)],
@@ -99,17 +104,18 @@
         for b, moved in enumerate(regroup(quad, 32 * tiles)):
             moved = moved.astype(BF)
             for D in range(tiles // 4):
-                out_ref[4 * D + b, 16 * at : 16 * at + 16] = moved[:, 128 * D : 128 * D + 128]
-
-
-def power_kernel(half_ref, weight_ref, table_ref, out_ref):
+                out_ref[goes[4 * D + b], 16 * at : 16 * at + 16] = moved[:, 128 * D : 128 * D + 128]
+
+
+def power_kernel(half_ref, weight_ref, table_ref, out_ref, *, came, goes):
     tiles = half_ref.shape[0]
     conds, kerns = weight_ref.shape
-    quad = [half_ref[:, 16 * q : 16 * q + 16, :].reshape(16 * tiles, 128).T for q in range(3)]
+    half = [half_ref[came[t]] for t in range(tiles)]
+    quad = [jnp.concatenate([h[16 * q : 16 * q + 16] for h in half], axis=0).T for q in range(3)]
     half_re = jnp.concatenate([quad[0], quad[2][:64]], axis=0)
     half_im = jnp.concatenate([quad[1], quad[2][64:]], axis=0)
-    field_re = dot(jnp.concatenate([half_re, -half_im], axis=1), table_ref[...], NT)
-    field_im = dot(jnp.concatenate([half_im, half_re], axis=1), table_ref[...], NT)
+    field_re = dot(jnp.concatenate([half_re, -half_im], axis=1), table_ref[...], NN)
+    field_im = dot(jnp.concatenate([half_im, half_re], axis=1), table_ref[...], NN)
     power = field_re * field_re + field_im * field_im
     for c in range(conds):
         total = None
@@ -120,34 +126,43 @@
         total = total.astype(BF)
         for d in range(out_ref.shape[0]):
             at = d % (total.shape[1] // 128) * 128
-            out_ref[d, 32 * c : 32 * c + 32] = total[:, at : at + 128]
-
-
-def bounds_kernel(parts_ref, low_ref, high_ref):
+            out_ref[goes[d], 32 * c : 32 * c + 32] = total[:, at : at + 128]
+
+
+def bounds_kernel(parts_ref, low_ref, high_ref, *, came):
     halves = []
     kern = parts_ref.shape[0] // 2
     for group in range(2):
-        total = parts_ref[group * kern].astype(F32)
+        total = parts_ref[came[group * kern]].astype(F32)
         for s in range(1, kern):
-            total = total + parts_ref[group * kern + s].astype(F32)
+            total = total + parts_ref[came[group * kern + s]].astype(F32)
         halves += [total[:32], total[32:]]
     low_ref[...] = jnp.minimum(jnp.minimum(halves[0], halves[1]), jnp.minimum(halves[2], halves[3]))
     high_ref[...] = jnp.maximum(jnp.maximum(halves[0], halves[1]), jnp.maximum(halves[2], halves[3]))
 
 
-def call(body, shapes, *args, spaces={}, scratch=(), cost=None):
+def call(body, shapes, *args, spaces={}, scratch=(), **places):
     return pl.pallas_call(
-        body,
+        functools.partial(body, **places),
         out_shape=shapes,
         in_specs=[
             pl.BlockSpec(memory_space=spaces.get(n, pltpu.VMEM)) for n in range(len(args))
         ],
         out_specs=jax.tree.map(lambda _: pl.BlockSpec(memory_space=pltpu.VMEM), shapes),
         scratch_shapes=scratch,
-        cost_estimate=cost,
         compiler_params=pltpu.CompilerParams(vmem_limit_bytes=48 * 1024 * 1024),
         name=body.__name__,
     )(*args)
+
+
+def swapped(blocks, axis, order):
+    return lax.all_to_all(
+        blocks, axis, split_axis=0, concat_axis=0, tiled=True, axis_index_groups=[order]
+    )
+
+
+def place(order):
+    return [order.index(member) for member in range(len(order))]
 
 
 def local(mask, kernels, kernel_weights):
@@ -156,8 +171,9 @@
     count = kernels.shape[4]
     tiles, groups = lax.axis_size("tile"), lax.axis_size("kern") * lax.axis_size("cond")
     cos_table, sin_table = tables(pixels, count)
-    table = jnp.asarray(np.concatenate([cos_table, sin_table], axis=1))
-    order = np.arange(count).reshape(tiles, 2, 8).transpose(1, 0, 2).reshape(-1)
+    table = jnp.asarray(np.concatenate([cos_table, sin_table], axis=1).T)
+    tile_order, image_order = rotated(tiles, 3 * tiles // 4), rotated(groups, 3 * groups // 4)
+    order = np.arange(count).reshape(tiles, 2, 8)[tile_order].transpose(1, 0, 2).reshape(-1)
     row_table = np.concatenate([cos_table[:, order], -sin_table[:, order]], axis=1)
     row_table = jnp.asarray(row_table[: pixels // 2])
     shape = jax.ShapeDtypeStruct
@@ -174,14 +190,29 @@
             pltpu.SemaphoreType.DMA((4,)),
         ],
     )
-    cols = lax.all_to_all(sent, "tile", split_axis=0, concat_axis=0, tiled=True)
-    half = call(half_kernel, shape((tiles, 48, 128), BF), cols, kern, table)
-    half = lax.all_to_all(half, "tile", split_axis=0, concat_axis=0, tiled=True)
+    cols = swapped(sent, "tile", tile_order)
+    half = call(
+        half_kernel,
+        shape((tiles, 48, 128), BF),
+        cols,
+        kern,
+        table,
+        came=place(tile_order),
+        goes=place(tile_order),
+    )
+    half = swapped(half, "tile", tile_order)
     weighted = call(
-        power_kernel, shape((groups, 64, 128), BF), half, kernel_weights, table, spaces={1: pltpu.SMEM}
-    )
-    parts = lax.all_to_all(weighted, ("cond", "kern"), split_axis=0, concat_axis=0, tiled=True)
-    low, high = call(bounds_kernel, (shape((32, 128), F32),) * 2, parts)
+        power_kernel,
+        shape((groups, 64, 128), BF),
+        half,
+        kernel_weights,
+        table,
+        spaces={1: pltpu.SMEM},
+        came=place(tile_order),
+        goes=place(image_order),
+    )
+    parts = swapped(weighted, ("cond", "kern"), image_order)
+    low, high = call(bounds_kernel, (shape((32, 128), F32),) * 2, parts, came=place(image_order))
     return (low[None], high[None])
 
 

time: 83.2 us -> 74.9 us (0.900)
  blocking collectives: 76.1 us -> 68.3 us
    all_to_all x3, blocking collectives: 76.1 us -> 68.3 us  [swapped(): lax.all_to_all(blocks, axis, split_axis=0, concat_axis=0, tiled=True, axi...]
where the time goes in v2:
time: 74.9 us; the launch traced here: 74.7 us
  blocking collectives  68.3 us (91%)
  Pallas kernels  5.74 us (8%)
    all_to_all x3, blocking collectives, swapped(): lax.all_to_all(blocks, axis, split_axis=0, concat_axis=0, tiled=True, axi...  68.3 us
    pallas_call x4, Pallas kernels, call(): pl.pallas_call(functools.partial(body, **places), out_shape=shapes, in_sp...  5.74 us

profile of v2, /device:TPU:1, one launch (start us, length us, event | category | flops | bytes accessed | tf_op | source)
XLA Modules:
  0.0 74.7 jit_solution(390161701515295905)
XLA Ops:
  0.6 2.0 %rows_kernel.1 = (bf16[256,128]{1,0:T(8,128)(2,1)S(1)}, bf16[1024,1024]{1,0:T(8,128)(2,1)S(1)}, bf16[2,6,16,512]{3,2,1,0:T(8,128)(2,1)S(1)}) custom-call(bf16[32,1024]{1,0:T(8,128)(2,1)} %bitcast.9, bf16[512,1024]{1,0:T(8,128)(2,1)} %constant.5.clone.rows_ref, bf16[1024,1024]{1,0:T(8,128)(2,1)} %constant.4.clone.table_ref, bf16[2,6,16,512]{3,2,1,0:T(8,128)(2,1)} %bitcast.8), custom_call_target="tpu_custom_call" | custom-call | tf_op jit(solution)/shard_map/rows_kernel/pallas_call | solution.py:145
  2.6 0.0 copy-start
  2.6 23.0 %all_to_all.21 = bf16[32,8,128]{2,1,0:T(8,128)(2,1)S(1)} all-to-all(bf16[32,8,128]{2,1,0:T(8,128)(2,1)S(1)} %bitcast.7), channel_id=1, replica_groups={{24,25,26,27,28,29,30,31,0,1,2,3,4,5,6,7,8,9,10,11,12,13,14,15,16,17,18..., dimensions={0} | all-to-all | bytes 131072 | tf_op jit(solution)/shard_map/all_to_all | solution.py:159
  25.7 1.5 %half_kernel.1 = bf16[32,48,128]{2,1,0:T(8,128)(2,1)S(1)} custom-call(bf16[256,128]{1,0:T(8,128)(2,1)S(1)} %bitcast.6, bf16[2,6,16,512]{3,2,1,0:T(8,128)(2,1)S(1)} %get-tuple-element.8.kern_ref, bf16[1024,1024]{1,0:T(8,128)(2,1)S(1)} %get-tuple-element.9.table_ref), custom_call_target="tpu_custom_call" | custom-call | tf_op jit(solution)/shard_map/half_kernel/pallas_call | solution.py:145
  27.2 29.7 %all_to_all.22.half_ref = bf16[32,48,128]{2,1,0:T(8,128)(2,1)S(1)} all-to-all(bf16[32,48,128]{2,1,0:T(8,128)(2,1)S(1)} %half_kernel.1), channel_id=1, replica_groups={{24,25,26,27,28,29,30,31,0,1,2,3,4,5,6,7,8,9,10,11,12,13,14,15,16,17,18..., dimensions={0} | all-to-all | bytes 786432 | tf_op jit(solution)/shard_map/all_to_all | solution.py:159
  56.9 0.0 copy-done
  56.9 1.6 %power_kernel.1 = bf16[16,64,128]{2,1,0:T(8,128)(2,1)S(1)} custom-call(bf16[32,48,128]{2,1,0:T(8,128)(2,1)S(1)} %all_to_all.22.half_ref, f32[2,3]{1,0:T(2,128)S(1)} %copy-done, bf16[1024,1024]{1,0:T(8,128)(2,1)S(1)} %get-tuple-element.9.table_ref), custom_call_target="tpu_custom_call" | custom-call | tf_op jit(solution)/shard_map/power_kernel/pallas_call | solution.py:145
  58.5 15.5 %all_to_all.23.parts_ref = bf16[16,64,128]{2,1,0:T(8,128)(2,1)S(1)} all-to-all(bf16[16,64,128]{2,1,0:T(8,128)(2,1)S(1)} %power_kernel.1), channel_id=1, replica_groups={{384,416,448,480,0,32,64,96,128,160,192,224,256,288,320,352},{385,417,4..., dimensions={0} | all-to-all | bytes 524288 | tf_op jit(solution)/shard_map/all_to_all | solution.py:159
  74.0 0.7 bounds_kernel.1
Async XLA Ops:
  2.6 54.3 %copy-start = (f32[2,3]{1,0:T(2,128)S(1)}, f32[2,3]{1,0:T(2,128)}, u32[]{:S(2)}) copy-start(f32[2,3]{1,0:T(2,128)} %weight_ref.1) | copy-start | bytes 76

commit v3 on v2

--- a/solution.py
+++ b/solution.py
@@ -16,8 +16,12 @@
 NT = (((1,), (1,)), ((), ()))
 
 
-def rotated(count, first):
-    return [(first + at) % count for at in range(count)]
+def ring_order(rings, length, first, step):
+    return [
+        ring * length + (first + step * at) % length
+        for at in range(length)
+        for ring in reversed(range(rings))
+    ]
 
 
 def tables(length, count):
@@ -29,6 +33,11 @@
         (np.cos(phase) * factor).astype(BF),
         (np.sin(phase) * factor).astype(BF),
     )
+
+
+def alternated(a):
+    odd = lax.broadcasted_iota(jnp.int32, a.shape, 1) % 2 == 1
+    return jnp.where(odd, -a, a)
 
 
 def dot(a, b, dims):
@@ -62,8 +71,7 @@
     half = pixels // 2
     both = jnp.concatenate([mask_buf[:, :half], mask_buf[:, half:]], axis=0)
     part = dot(both, table_buf[...], NN)
-    odd = lax.broadcasted_iota(jnp.int32, (rows, part.shape[1]), 1) % 2 == 1
-    out = part[:rows] + jnp.where(odd, -part[rows:], part[rows:])
+    out = part[:rows] + alternated(part[rows:])
     width = out.shape[1] // 4
     stacked = jnp.concatenate([out[:, g * width : (g + 1) * width] for g in range(4)], axis=0)
     out_ref[...] = stacked.T.astype(BF)
@@ -80,7 +88,9 @@
     ]
     groups = regroup(blocks, 32 * tiles)
     lines = jnp.concatenate(groups, axis=0).astype(BF)
-    part = dot(lines, table_ref[...], NT)
+    near = lines.shape[1] // 2
+    part = dot(jnp.concatenate([lines[:, :near], lines[:, near:]], axis=0), table_ref[...], NT)
+    part = part[:32] + alternated(part[32:])
     spec_re = part[:16, :count] + part[16:, count:]
     spec_im = part[16:, :count] - part[:16, count:]
     top, low = [], []
@@ -93,18 +103,17 @@
         top.append(jnp.concatenate([fre, -fim], axis=1))
         low.append(jnp.concatenate([fim, fre], axis=1))
     lhs = jnp.concatenate(top + low, axis=0)
-    fields = dot(lhs, table_ref[...], NN)
-    pick = lambda ri, n: fields[(ri * items + n) * 16 : (ri * items + n + 1) * 16]
-    quads = (
-        [pick(0, n) for n in range(4)],
-        [pick(1, n) for n in range(4)],
-        [pick(0, 4), pick(0, 5), pick(1, 4), pick(1, 5)],
-    )
-    for at, quad in enumerate(quads):
-        for b, moved in enumerate(regroup(quad, 32 * tiles)):
-            moved = moved.astype(BF)
-            for D in range(tiles // 4):
-                out_ref[goes[4 * D + b], 16 * at : 16 * at + 16] = moved[:, 128 * D : 128 * D + 128]
+    fields = dot(jnp.concatenate([lhs, alternated(lhs)], axis=0), table_ref[...], NN)
+    for side in range(2):
+        start = side * lhs.shape[0]
+        block = [fields[start + 16 * n : start + 16 * n + 16] for n in range(2 * items)]
+        quads = (block[:4], block[items : items + 4], block[4:items] + block[items + 4 :])
+        for at, quad in enumerate(quads):
+            for b, moved in enumerate(regroup(quad, near)):
+                moved = moved.astype(BF)
+                for D in range(near // 128):
+                    d = side * tiles // 2 + 4 * D + b
+                    out_ref[goes[d], 16 * at : 16 * at + 16] = moved[:, 128 * D : 128 * D + 128]
 
 
 def power_kernel(half_ref, weight_ref, table_ref, out_ref, *, came, goes):
@@ -114,19 +123,27 @@
     quad = [jnp.concatenate([h[16 * q : 16 * q + 16] for h in half], axis=0).T for q in range(3)]
     half_re = jnp.concatenate([quad[0], quad[2][:64]], axis=0)
     half_im = jnp.concatenate([quad[1], quad[2][64:]], axis=0)
-    field_re = dot(jnp.concatenate([half_re, -half_im], axis=1), table_ref[...], NN)
-    field_im = dot(jnp.concatenate([half_im, half_re], axis=1), table_ref[...], NN)
-    power = field_re * field_re + field_im * field_im
-    for c in range(conds):
-        total = None
-        for k in range(kerns):
-            n = c * kerns + k
-            term = power[32 * n : 32 * n + 32] * weight_ref[c, k]
-            total = term if total is None else total + term
-        total = total.astype(BF)
-        for d in range(out_ref.shape[0]):
-            at = d % (total.shape[1] // 128) * 128
-            out_ref[goes[d], 32 * c : 32 * c + 32] = total[:, at : at + 128]
+    lhs_re = jnp.concatenate([half_re, -half_im], axis=1)
+    lhs_im = jnp.concatenate([half_im, half_re], axis=1)
+    lhs = jnp.concatenate([lhs_re, lhs_im, alternated(lhs_re), alternated(lhs_im)], axis=0)
+    fields = dot(lhs, table_ref[...], NN)
+    count = half_re.shape[0]
+    near = fields.shape[1] // 128
+    for side in range(2):
+        field_re = fields[2 * side * count : (2 * side + 1) * count]
+        field_im = fields[(2 * side + 1) * count : (2 * side + 2) * count]
+        power = field_re * field_re + field_im * field_im
+        for c in range(conds):
+            total = None
+            for k in range(kerns):
+                n = c * kerns + k
+                term = power[32 * n : 32 * n + 32] * weight_ref[c, k]
+                total = term if total is None else total + term
+            total = total.astype(BF)
+            for d in range(out_ref.shape[0]):
+                if d % (2 * near) // near == side:
+                    at = d % near * 128
+                    out_ref[goes[d], 32 * c : 32 * c + 32] = total[:, at : at + 128]
 
 
 def bounds_kernel(parts_ref, low_ref, high_ref, *, came):
@@ -171,8 +188,9 @@
     count = kernels.shape[4]
     tiles, groups = lax.axis_size("tile"), lax.axis_size("kern") * lax.axis_size("cond")
     cos_table, sin_table = tables(pixels, count)
-    table = jnp.asarray(np.concatenate([cos_table, sin_table], axis=1).T)
-    tile_order, image_order = rotated(tiles, 3 * tiles // 4), rotated(groups, 3 * groups // 4)
+    table = jnp.asarray(np.concatenate([cos_table, sin_table], axis=1)[: pixels // 2].T)
+    tile_order = ring_order(2, tiles // 2, 10, 7)
+    image_order = ring_order(1, groups, 13, 1)
     order = np.arange(count).reshape(tiles, 2, 8)[tile_order].transpose(1, 0, 2).reshape(-1)
     row_table = np.concatenate([cos_table[:, order], -sin_table[:, order]], axis=1)
     row_table = jnp.asarray(row_table[: pixels // 2])

time: 74.9 us -> 71.6 us (0.956)
  blocking collectives: 68.3 us -> 65.4 us
    all_to_all x3, blocking collectives: 68.3 us -> 65.4 us  [swapped(): lax.all_to_all(blocks, axis, split_axis=0, concat_axis=0, tiled=True, axi...]
where the time goes in v3:
time: 71.6 us; the launch traced here: 71.3 us
  blocking collectives  65.4 us (91%)
  Pallas kernels  5.25 us (7%)
    all_to_all x3, blocking collectives, swapped(): lax.all_to_all(blocks, axis, split_axis=0, concat_axis=0, tiled=True, axi...  65.4 us
    pallas_call x4, Pallas kernels, call(): pl.pallas_call(functools.partial(body, **places), out_shape=shapes, in_sp...  5.25 us

profile of v3, /device:TPU:1, one launch (start us, length us, event | category | flops | bytes accessed | tf_op | source)
XLA Modules:
  0.0 71.3 jit_solution(6757783528476286468)
XLA Ops:
  0.6 1.7 %rows_kernel.1 = (bf16[256,128]{1,0:T(8,128)(2,1)S(1)}, bf16[1024,512]{1,0:T(8,128)(2,1)S(1)}, bf16[2,6,16,512]{3,2,1,0:T(8,128)(2,1)S(1)}) custom-call(bf16[32,1024]{1,0:T(8,128)(2,1)} %bitcast.9, bf16[512,1024]{1,0:T(8,128)(2,1)} %constant.5.clone.rows_ref, bf16[1024,512]{1,0:T(8,128)(2,1)} %constant.4.clone.table_ref, bf16[2,6,16,512]{3,2,1,0:T(8,128)(2,1)} %bitcast.8), custom_call_target="tpu_custom_call" | custom-call | tf_op jit(solution)/shard_map/rows_kernel/pallas_call | solution.py:162
  2.3 22.8 %all_to_all.21 = bf16[32,8,128]{2,1,0:T(8,128)(2,1)S(1)} all-to-all(bf16[32,8,128]{2,1,0:T(8,128)(2,1)S(1)} %bitcast.7), channel_id=1, replica_groups={{26,10,17,1,24,8,31,15,22,6,29,13,20,4,27,11,18,2,25,9,16,0,23,7,30,14,..., dimensions={0} | all-to-all | bytes 131072 | tf_op jit(solution)/shard_map/all_to_all | solution.py:176
  25.2 1.3 %half_kernel.1 = bf16[32,48,128]{2,1,0:T(8,128)(2,1)S(1)} custom-call(bf16[256,128]{1,0:T(8,128)(2,1)S(1)} %bitcast.6, bf16[2,6,16,512]{3,2,1,0:T(8,128)(2,1)S(1)} %get-tuple-element.8.kern_ref, bf16[1024,512]{1,0:T(8,128)(2,1)S(1)} %get-tuple-element.9.table_ref), custom_call_target="tpu_custom_call" | custom-call | tf_op jit(solution)/shard_map/half_kernel/pallas_call | solution.py:162
  26.5 0.0 copy-start
  26.5 26.3 %all_to_all.22.half_ref = bf16[32,48,128]{2,1,0:T(8,128)(2,1)S(1)} all-to-all(bf16[32,48,128]{2,1,0:T(8,128)(2,1)S(1)} %half_kernel.1), channel_id=1, replica_groups={{26,10,17,1,24,8,31,15,22,6,29,13,20,4,27,11,18,2,25,9,16,0,23,7,30,14,..., dimensions={0} | all-to-all | bytes 786432 | tf_op jit(solution)/shard_map/all_to_all | solution.py:176
  52.8 0.0 copy-done
  52.8 1.6 %power_kernel.1 = bf16[16,64,128]{2,1,0:T(8,128)(2,1)S(1)} custom-call(bf16[32,48,128]{2,1,0:T(8,128)(2,1)S(1)} %all_to_all.22.half_ref, f32[2,3]{1,0:T(2,128)S(1)} %copy-done, bf16[1024,512]{1,0:T(8,128)(2,1)S(1)} %get-tuple-element.9.table_ref), custom_call_target="tpu_custom_call" | custom-call | tf_op jit(solution)/shard_map/power_kernel/pallas_call | solution.py:162
  54.4 16.3 %all_to_all.23.parts_ref = bf16[16,64,128]{2,1,0:T(8,128)(2,1)S(1)} all-to-all(bf16[16,64,128]{2,1,0:T(8,128)(2,1)S(1)} %power_kernel.1), channel_id=1, replica_groups={{416,448,480,0,32,64,96,128,160,192,224,256,288,320,352,384},{417,449,4..., dimensions={0} | all-to-all | bytes 524288 | tf_op jit(solution)/shard_map/all_to_all | solution.py:176
  70.7 0.7 bounds_kernel.1
Async XLA Ops:
  26.5 26.3 %copy-start = (f32[2,3]{1,0:T(2,128)S(1)}, f32[2,3]{1,0:T(2,128)}, u32[]{:S(2)}) copy-start(f32[2,3]{1,0:T(2,128)} %weight_ref.1) | copy-start | bytes 76

commit v4 on v3

--- a/solution.py
+++ b/solution.py
@@ -35,9 +35,34 @@
     )
 
 
-def alternated(a):
-    odd = lax.broadcasted_iota(jnp.int32, a.shape, 1) % 2 == 1
-    return jnp.where(odd, -a, a)
+def turned(re, im, quarters):
+    quarters %= 4
+    if quarters == 0:
+        return re, im
+    place = lax.broadcasted_iota(jnp.int32, re.shape, 1) % 4
+    odd = place % 2 == 1
+    if quarters == 2:
+        return jnp.where(odd, -re, re), jnp.where(odd, -im, im)
+    real, imag = jnp.where(odd, im, re), jnp.where(odd, re, im)
+    early, late = (place == 1) | (place == 2), place >= 2
+    if quarters == 3:
+        early, late = late, early
+    return jnp.where(early, -real, real), jnp.where(late, -imag, imag)
+
+
+def summed(pairs):
+    total_re, total_im = pairs[0]
+    for re, im in pairs[1:]:
+        total_re, total_im = total_re + re, total_im + im
+    return total_re, total_im
+
+
+def sided(re, im):
+    rows = []
+    for m in range(4):
+        there_re, there_im = turned(re, im, m)
+        rows += [jnp.concatenate([there_re, -there_im], axis=1), jnp.concatenate([there_im, there_re], axis=1)]
+    return jnp.concatenate(rows, axis=0)
 
 
 def dot(a, b, dims):
@@ -68,10 +93,14 @@
     for copy in copies[:2]:
         copy.wait()
     rows, pixels = mask_buf.shape
-    half = pixels // 2
-    both = jnp.concatenate([mask_buf[:, :half], mask_buf[:, half:]], axis=0)
+    near = pixels // 4
+    both = jnp.concatenate([mask_buf[:, m * near : (m + 1) * near] for m in range(4)], axis=0)
     part = dot(both, table_buf[...], NN)
-    out = part[:rows] + alternated(part[rows:])
+    count = part.shape[1] // 2
+    parts = [part[m * rows : (m + 1) * rows] for m in range(4)]
+    out = jnp.concatenate(
+        summed([turned(p[:, :count], p[:, count:], -m) for m, p in enumerate(parts)]), axis=1
+    )
     width = out.shape[1] // 4
     stacked = jnp.concatenate([out[:, g * width : (g + 1) * width] for g in range(4)], axis=0)
     out_ref[...] = stacked.T.astype(BF)
@@ -88,31 +117,34 @@
     ]
     groups = regroup(blocks, 32 * tiles)
     lines = jnp.concatenate(groups, axis=0).astype(BF)
-    near = lines.shape[1] // 2
-    part = dot(jnp.concatenate([lines[:, :near], lines[:, near:]], axis=0), table_ref[...], NT)
-    part = part[:32] + alternated(part[32:])
-    spec_re = part[:16, :count] + part[16:, count:]
-    spec_im = part[16:, :count] - part[:16, count:]
-    top, low = [], []
+    near = lines.shape[1] // 4
+    lines = jnp.concatenate([lines[:, m * near : (m + 1) * near] for m in range(4)], axis=0)
+    part = dot(lines, table_ref[...], NT)
+    parts = []
+    for m in range(4):
+        top, low = part[32 * m : 32 * m + 16], part[32 * m + 16 : 32 * m + 32]
+        parts.append(
+            turned(top[:, :count] + low[:, count:], low[:, :count] - top[:, count:], -m)
+        )
+    spec_re, spec_im = summed(parts)
     items = kern_ref.shape[1]
+    fre, fim = [], []
     for n in range(items):
         kre = kern_ref[0, n].astype(F32)
         kim = kern_ref[1, n].astype(F32)
-        fre = (spec_re * kre - spec_im * kim).astype(BF)
-        fim = (spec_re * kim + spec_im * kre).astype(BF)
-        top.append(jnp.concatenate([fre, -fim], axis=1))
-        low.append(jnp.concatenate([fim, fre], axis=1))
-    lhs = jnp.concatenate(top + low, axis=0)
-    fields = dot(jnp.concatenate([lhs, alternated(lhs)], axis=0), table_ref[...], NN)
-    for side in range(2):
-        start = side * lhs.shape[0]
+        fre.append((spec_re * kre - spec_im * kim).astype(BF))
+        fim.append((spec_re * kim + spec_im * kre).astype(BF))
+    lhs = sided(jnp.concatenate(fre, axis=0), jnp.concatenate(fim, axis=0))
+    fields = dot(lhs, table_ref[...], NN)
+    for side in range(4):
+        start = side * 32 * items
         block = [fields[start + 16 * n : start + 16 * n + 16] for n in range(2 * items)]
         quads = (block[:4], block[items : items + 4], block[4:items] + block[items + 4 :])
         for at, quad in enumerate(quads):
             for b, moved in enumerate(regroup(quad, near)):
                 moved = moved.astype(BF)
                 for D in range(near // 128):
-                    d = side * tiles // 2 + 4 * D + b
+                    d = side * tiles // 4 + 4 * D + b
                     out_ref[goes[d], 16 * at : 16 * at + 16] = moved[:, 128 * D : 128 * D + 128]
 
 
@@ -123,13 +155,10 @@
     quad = [jnp.concatenate([h[16 * q : 16 * q + 16] for h in half], axis=0).T for q in range(3)]
     half_re = jnp.concatenate([quad[0], quad[2][:64]], axis=0)
     half_im = jnp.concatenate([quad[1], quad[2][64:]], axis=0)
-    lhs_re = jnp.concatenate([half_re, -half_im], axis=1)
-    lhs_im = jnp.concatenate([half_im, half_re], axis=1)
-    lhs = jnp.concatenate([lhs_re, lhs_im, alternated(lhs_re), alternated(lhs_im)], axis=0)
-    fields = dot(lhs, table_ref[...], NN)
+    fields = dot(sided(half_re, half_im), table_ref[...], NN)
     count = half_re.shape[0]
     near = fields.shape[1] // 128
-    for side in range(2):
+    for side in range(4):
         field_re = fields[2 * side * count : (2 * side + 1) * count]
         field_im = fields[(2 * side + 1) * count : (2 * side + 2) * count]
         power = field_re * field_re + field_im * field_im
@@ -141,7 +170,7 @@
                 total = term if total is None else total + term
             total = total.astype(BF)
             for d in range(out_ref.shape[0]):
-                if d % (2 * near) // near == side:
+                if d % (4 * near) // near == side:
                     at = d % near * 128
                     out_ref[goes[d], 32 * c : 32 * c + 32] = total[:, at : at + 128]
 
@@ -188,12 +217,12 @@
     count = kernels.shape[4]
     tiles, groups = lax.axis_size("tile"), lax.axis_size("kern") * lax.axis_size("cond")
     cos_table, sin_table = tables(pixels, count)
-    table = jnp.asarray(np.concatenate([cos_table, sin_table], axis=1)[: pixels // 2].T)
+    table = jnp.asarray(np.concatenate([cos_table, sin_table], axis=1)[: pixels // 4].T)
     tile_order = ring_order(2, tiles // 2, 10, 7)
     image_order = ring_order(1, groups, 13, 1)
     order = np.arange(count).reshape(tiles, 2, 8)[tile_order].transpose(1, 0, 2).reshape(-1)
     row_table = np.concatenate([cos_table[:, order], -sin_table[:, order]], axis=1)
-    row_table = jnp.asarray(row_table[: pixels // 2])
+    row_table = jnp.asarray(row_table[: pixels // 4])
     shape = jax.ShapeDtypeStruct
 
     kern = kernels.reshape(2, conds * kerns, kernels.shape[3], count)

time: 71.6 us -> 71.3 us (level)
  no operation moved by 1% of the time
where the time goes in v4:
time: 71.3 us; the launch traced here: 71.1 us
  blocking collectives  65.4 us (92%)
  Pallas kernels  4.95 us (7%)
    all_to_all x3, blocking collectives, swapped(): lax.all_to_all(blocks, axis, split_axis=0, concat_axis=0, tiled=True, axi...  65.4 us
    pallas_call x4, Pallas kernels, call(): pl.pallas_call(functools.partial(body, **places), out_shape=shapes, in_sp...  4.95 us

profile of v4, /device:TPU:1, one launch (start us, length us, event | category | flops | bytes accessed | tf_op | source)
XLA Modules:
  0.0 71.1 jit_solution(6217585334328038456)
XLA Ops:
  0.6 1.5 %rows_kernel.1 = (bf16[256,128]{1,0:T(8,128)(2,1)S(1)}, bf16[1024,256]{1,0:T(8,128)(2,1)S(1)}, bf16[2,6,16,512]{3,2,1,0:T(8,128)(2,1)S(1)}) custom-call(bf16[32,1024]{1,0:T(8,128)(2,1)} %bitcast.9, bf16[256,1024]{1,0:T(8,128)(2,1)} %constant.5.clone.rows_ref, bf16[1024,256]{1,0:T(8,128)(2,1)} %constant.4.clone.table_ref, bf16[2,6,16,512]{3,2,1,0:T(8,128)(2,1)} %bitcast.8), custom_call_target="tpu_custom_call" | custom-call | tf_op jit(solution)/shard_map/rows_kernel/pallas_call | solution.py:191
  2.1 22.8 %all_to_all.21 = bf16[32,8,128]{2,1,0:T(8,128)(2,1)S(1)} all-to-all(bf16[32,8,128]{2,1,0:T(8,128)(2,1)S(1)} %bitcast.7), channel_id=1, replica_groups={{26,10,17,1,24,8,31,15,22,6,29,13,20,4,27,11,18,2,25,9,16,0,23,7,30,14,..., dimensions={0} | all-to-all | bytes 131072 | tf_op jit(solution)/shard_map/all_to_all | solution.py:205
  24.9 1.3 %half_kernel.1 = bf16[32,48,128]{2,1,0:T(8,128)(2,1)S(1)} custom-call(bf16[256,128]{1,0:T(8,128)(2,1)S(1)} %bitcast.6, bf16[2,6,16,512]{3,2,1,0:T(8,128)(2,1)S(1)} %get-tuple-element.8.kern_ref, bf16[1024,256]{1,0:T(8,128)(2,1)S(1)} %get-tuple-element.9.table_ref), custom_call_target="tpu_custom_call" | custom-call | tf_op jit(solution)/shard_map/half_kernel/pallas_call | solution.py:191
  26.2 0.0 copy-start
  26.2 26.3 %all_to_all.22.half_ref = bf16[32,48,128]{2,1,0:T(8,128)(2,1)S(1)} all-to-all(bf16[32,48,128]{2,1,0:T(8,128)(2,1)S(1)} %half_kernel.1), channel_id=1, replica_groups={{26,10,17,1,24,8,31,15,22,6,29,13,20,4,27,11,18,2,25,9,16,0,23,7,30,14,..., dimensions={0} | all-to-all | bytes 786432 | tf_op jit(solution)/shard_map/all_to_all | solution.py:205
  52.6 0.0 copy-done
  52.6 1.6 %power_kernel.1 = bf16[16,64,128]{2,1,0:T(8,128)(2,1)S(1)} custom-call(bf16[32,48,128]{2,1,0:T(8,128)(2,1)S(1)} %all_to_all.22.half_ref, f32[2,3]{1,0:T(2,128)S(1)} %copy-done, bf16[1024,256]{1,0:T(8,128)(2,1)S(1)} %get-tuple-element.9.table_ref), custom_call_target="tpu_custom_call" | custom-call | tf_op jit(solution)/shard_map/power_kernel/pallas_call | solution.py:191
  54.1 16.3 %all_to_all.23.parts_ref = bf16[16,64,128]{2,1,0:T(8,128)(2,1)S(1)} all-to-all(bf16[16,64,128]{2,1,0:T(8,128)(2,1)S(1)} %power_kernel.1), channel_id=1, replica_groups={{416,448,480,0,32,64,96,128,160,192,224,256,288,320,352,384},{417,449,4..., dimensions={0} | all-to-all | bytes 524288 | tf_op jit(solution)/shard_map/all_to_all | solution.py:205
  70.4 0.7 bounds_kernel.1
Async XLA Ops:
  26.2 26.4 %copy-start = (f32[2,3]{1,0:T(2,128)S(1)}, f32[2,3]{1,0:T(2,128)}, u32[]{:S(2)}) copy-start(f32[2,3]{1,0:T(2,128)} %weight_ref.1) | copy-start | bytes 76

commit v5 on v4

--- a/solution.py
+++ b/solution.py
@@ -88,8 +88,10 @@
 ):
     pairs = [(mask_ref, mask_buf), (rows_ref, table_buf), (table_ref, table_out), (kern_ref, kern_out)]
     copies = [pltpu.make_async_copy(src, dst, sems.at[n]) for n, (src, dst) in enumerate(pairs)]
-    for copy in copies:
+    for copy in copies[:2]:
         copy.start()
+    for copy in copies[2:]:
+        copy.start(priority=1)
     for copy in copies[:2]:
         copy.wait()
     rows, pixels = mask_buf.shape
@@ -219,8 +221,9 @@
     cos_table, sin_table = tables(pixels, count)
     table = jnp.asarray(np.concatenate([cos_table, sin_table], axis=1)[: pixels // 4].T)
     tile_order = ring_order(2, tiles // 2, 10, 7)
+    rows_order = ring_order(2, tiles // 2, 11, 7)
     image_order = ring_order(1, groups, 13, 1)
-    order = np.arange(count).reshape(tiles, 2, 8)[tile_order].transpose(1, 0, 2).reshape(-1)
+    order = np.arange(count).reshape(tiles, 2, 8)[rows_order].transpose(1, 0, 2).reshape(-1)
     row_table = np.concatenate([cos_table[:, order], -sin_table[:, order]], axis=1)
     row_table = jnp.asarray(row_table[: pixels // 4])
     shape = jax.ShapeDtypeStruct
@@ -237,14 +240,14 @@
             pltpu.SemaphoreType.DMA((4,)),
         ],
     )
-    cols = swapped(sent, "tile", tile_order)
+    cols = swapped(sent, "tile", rows_order)
     half = call(
         half_kernel,
         shape((tiles, 48, 128), BF),
         cols,
         kern,
         table,
-        came=place(tile_order),
+        came=place(rows_order),
         goes=place(tile_order),
     )
     half = swapped(half, "tile", tile_order)

time: 71.3 us -> 71 us (level)
    all_to_all x3, blocking collectives: 65.4 us -> 64.7 us  [swapped(): lax.all_to_all(blocks, axis, split_axis=0, concat_axis=0, tiled=True, axi...]
where the time goes in v5:
time: 71 us; the launch traced here: 70.3 us
  blocking collectives  64.7 us (91%)
  Pallas kernels  4.94 us (7%)
    all_to_all x3, blocking collectives, swapped(): lax.all_to_all(blocks, axis, split_axis=0, concat_axis=0, tiled=True, axi...  64.7 us
    pallas_call x4, Pallas kernels, call(): pl.pallas_call(functools.partial(body, **places), out_shape=shapes, in_sp...  4.94 us

profile of v5, /device:TPU:1, one launch (start us, length us, event | category | flops | bytes accessed | tf_op | source)
XLA Modules:
  0.0 70.3 jit_solution(5140909726839436953)
XLA Ops:
  0.6 1.5 %rows_kernel.1 = (bf16[256,128]{1,0:T(8,128)(2,1)S(1)}, bf16[1024,256]{1,0:T(8,128)(2,1)S(1)}, bf16[2,6,16,512]{3,2,1,0:T(8,128)(2,1)S(1)}) custom-call(bf16[32,1024]{1,0:T(8,128)(2,1)} %bitcast.9, bf16[256,1024]{1,0:T(8,128)(2,1)} %constant.5.clone.rows_ref, bf16[1024,256]{1,0:T(8,128)(2,1)} %constant.4.clone.table_ref, bf16[2,6,16,512]{3,2,1,0:T(8,128)(2,1)} %bitcast.8), custom_call_target="tpu_custom_call" | custom-call | tf_op jit(solution)/shard_map/rows_kernel/pallas_call | solution.py:193
  2.1 23.0 %all_to_all.21 = bf16[32,8,128]{2,1,0:T(8,128)(2,1)S(1)} all-to-all(bf16[32,8,128]{2,1,0:T(8,128)(2,1)S(1)} %bitcast.7), channel_id=1, replica_groups={{27,11,18,2,25,9,16,0,23,7,30,14,21,5,28,12,19,3,26,10,17,1,24,8,31,15,..., dimensions={0} | all-to-all | bytes 131072 | tf_op jit(solution)/shard_map/all_to_all | solution.py:207
  25.1 1.2 %half_kernel.1 = bf16[32,48,128]{2,1,0:T(8,128)(2,1)S(1)} custom-call(bf16[256,128]{1,0:T(8,128)(2,1)S(1)} %bitcast.6, bf16[2,6,16,512]{3,2,1,0:T(8,128)(2,1)S(1)} %get-tuple-element.8.kern_ref, bf16[1024,256]{1,0:T(8,128)(2,1)S(1)} %get-tuple-element.9.table_ref), custom_call_target="tpu_custom_call" | custom-call | tf_op jit(solution)/shard_map/half_kernel/pallas_call | solution.py:193
  26.4 0.0 copy-start
  26.4 26.4 %all_to_all.22.half_ref = bf16[32,48,128]{2,1,0:T(8,128)(2,1)S(1)} all-to-all(bf16[32,48,128]{2,1,0:T(8,128)(2,1)S(1)} %half_kernel.1), channel_id=1, replica_groups={{26,10,17,1,24,8,31,15,22,6,29,13,20,4,27,11,18,2,25,9,16,0,23,7,30,14,..., dimensions={0} | all-to-all | bytes 786432 | tf_op jit(solution)/shard_map/all_to_all | solution.py:207
  52.8 0.0 copy-done
  52.8 1.6 %power_kernel.1 = bf16[16,64,128]{2,1,0:T(8,128)(2,1)S(1)} custom-call(bf16[32,48,128]{2,1,0:T(8,128)(2,1)S(1)} %all_to_all.22.half_ref, f32[2,3]{1,0:T(2,128)S(1)} %copy-done, bf16[1024,256]{1,0:T(8,128)(2,1)S(1)} %get-tuple-element.9.table_ref), custom_call_target="tpu_custom_call" | custom-call | tf_op jit(solution)/shard_map/power_kernel/pallas_call | solution.py:193
  54.4 15.3 %all_to_all.23.parts_ref = bf16[16,64,128]{2,1,0:T(8,128)(2,1)S(1)} all-to-all(bf16[16,64,128]{2,1,0:T(8,128)(2,1)S(1)} %power_kernel.1), channel_id=1, replica_groups={{416,448,480,0,32,64,96,128,160,192,224,256,288,320,352,384},{417,449,4..., dimensions={0} | all-to-all | bytes 524288 | tf_op jit(solution)/shard_map/all_to_all | solution.py:207
  69.6 0.7 bounds_kernel.1
Async XLA Ops:
  26.4 26.4 %copy-start = (f32[2,3]{1,0:T(2,128)S(1)}, f32[2,3]{1,0:T(2,128)}, u32[]{:S(2)}) copy-start(f32[2,3]{1,0:T(2,128)} %weight_ref.1) | copy-start | bytes 76

commit v6 on v5

--- a/solution.py
+++ b/solution.py
@@ -87,12 +87,17 @@
     mask_ref, rows_ref, table_ref, kern_ref, out_ref, table_out, kern_out, mask_buf, table_buf, sems
 ):
     pairs = [(mask_ref, mask_buf), (rows_ref, table_buf), (table_ref, table_out), (kern_ref, kern_out)]
-    copies = [pltpu.make_async_copy(src, dst, sems.at[n]) for n, (src, dst) in enumerate(pairs)]
-    for copy in copies[:2]:
+    pieces = [(mask_ref, mask_buf)]
+    for src, dst in pairs[1:]:
+        step = src.shape[0] // 2
+        for at in (0, step):
+            pieces.append((src.at[pl.ds(at, step)], dst.at[pl.ds(at, step)]))
+    copies = [pltpu.make_async_copy(src, dst, sems.at[n]) for n, (src, dst) in enumerate(pieces)]
+    for copy in copies[:3]:
         copy.start()
-    for copy in copies[2:]:
+    for copy in copies[3:]:
         copy.start(priority=1)
-    for copy in copies[:2]:
+    for copy in copies[:3]:
         copy.wait()
     rows, pixels = mask_buf.shape
     near = pixels // 4
@@ -106,7 +111,7 @@
     width = out.shape[1] // 4
     stacked = jnp.concatenate([out[:, g * width : (g + 1) * width] for g in range(4)], axis=0)
     out_ref[...] = stacked.T.astype(BF)
-    for copy in copies[2:]:
+    for copy in copies[3:]:
         copy.wait()
 
 
@@ -237,7 +242,7 @@
         scratch=[
             pltpu.VMEM((rows, pixels), BF),
             pltpu.VMEM(row_table.shape, BF),
-            pltpu.SemaphoreType.DMA((4,)),
+            pltpu.SemaphoreType.DMA((7,)),
         ],
     )
     cols = swapped(sent, "tile", rows_order)

time: 71 us -> 71 us (level)
  no operation moved by 1% of the time
where the time goes in v6:
time: 71 us; the launch traced here: 70.3 us
  blocking collectives  64.7 us (91%)
  Pallas kernels  4.96 us (7%)
    all_to_all x3, blocking collectives, swapped(): lax.all_to_all(blocks, axis, split_axis=0, concat_axis=0, tiled=True, axi...  64.7 us
    pallas_call x4, Pallas kernels, call(): pl.pallas_call(functools.partial(body, **places), out_shape=shapes, in_sp...  4.96 us

profile of v6, /device:TPU:1, one launch (start us, length us, event | category | flops | bytes accessed | tf_op | source)
XLA Modules:
  0.0 70.3 jit_solution(8771118369456646636)
XLA Ops:
  0.6 1.5 %rows_kernel.1 = (bf16[256,128]{1,0:T(8,128)(2,1)S(1)}, bf16[1024,256]{1,0:T(8,128)(2,1)S(1)}, bf16[2,6,16,512]{3,2,1,0:T(8,128)(2,1)S(1)}) custom-call(bf16[32,1024]{1,0:T(8,128)(2,1)} %bitcast.9, bf16[256,1024]{1,0:T(8,128)(2,1)} %constant.5.clone.rows_ref, bf16[1024,256]{1,0:T(8,128)(2,1)} %constant.4.clone.table_ref, bf16[2,6,16,512]{3,2,1,0:T(8,128)(2,1)} %bitcast.8), custom_call_target="tpu_custom_call" | custom-call | tf_op jit(solution)/shard_map/rows_kernel/pallas_call | solution.py:198
  2.1 23.0 %all_to_all.21 = bf16[32,8,128]{2,1,0:T(8,128)(2,1)S(1)} all-to-all(bf16[32,8,128]{2,1,0:T(8,128)(2,1)S(1)} %bitcast.7), channel_id=1, replica_groups={{27,11,18,2,25,9,16,0,23,7,30,14,21,5,28,12,19,3,26,10,17,1,24,8,31,15,..., dimensions={0} | all-to-all | bytes 131072 | tf_op jit(solution)/shard_map/all_to_all | solution.py:212
  25.1 1.2 %half_kernel.1 = bf16[32,48,128]{2,1,0:T(8,128)(2,1)S(1)} custom-call(bf16[256,128]{1,0:T(8,128)(2,1)S(1)} %bitcast.6, bf16[2,6,16,512]{3,2,1,0:T(8,128)(2,1)S(1)} %get-tuple-element.8.kern_ref, bf16[1024,256]{1,0:T(8,128)(2,1)S(1)} %get-tuple-element.9.table_ref), custom_call_target="tpu_custom_call" | custom-call | tf_op jit(solution)/shard_map/half_kernel/pallas_call | solution.py:198
  26.4 0.0 copy-start
  26.4 26.4 %all_to_all.22.half_ref = bf16[32,48,128]{2,1,0:T(8,128)(2,1)S(1)} all-to-all(bf16[32,48,128]{2,1,0:T(8,128)(2,1)S(1)} %half_kernel.1), channel_id=1, replica_groups={{26,10,17,1,24,8,31,15,22,6,29,13,20,4,27,11,18,2,25,9,16,0,23,7,30,14,..., dimensions={0} | all-to-all | bytes 786432 | tf_op jit(solution)/shard_map/all_to_all | solution.py:212
  52.8 0.0 copy-done
  52.8 1.6 %power_kernel.1 = bf16[16,64,128]{2,1,0:T(8,128)(2,1)S(1)} custom-call(bf16[32,48,128]{2,1,0:T(8,128)(2,1)S(1)} %all_to_all.22.half_ref, f32[2,3]{1,0:T(2,128)S(1)} %copy-done, bf16[1024,256]{1,0:T(8,128)(2,1)S(1)} %get-tuple-element.9.table_ref), custom_call_target="tpu_custom_call" | custom-call | tf_op jit(solution)/shard_map/power_kernel/pallas_call | solution.py:198
  54.4 15.3 %all_to_all.23.parts_ref = bf16[16,64,128]{2,1,0:T(8,128)(2,1)S(1)} all-to-all(bf16[16,64,128]{2,1,0:T(8,128)(2,1)S(1)} %power_kernel.1), channel_id=1, replica_groups={{416,448,480,0,32,64,96,128,160,192,224,256,288,320,352,384},{417,449,4..., dimensions={0} | all-to-all | bytes 524288 | tf_op jit(solution)/shard_map/all_to_all | solution.py:212
  69.6 0.7 bounds_kernel.1
Async XLA Ops:
  26.4 26.4 %copy-start = (f32[2,3]{1,0:T(2,128)S(1)}, f32[2,3]{1,0:T(2,128)}, u32[]{:S(2)}) copy-start(f32[2,3]{1,0:T(2,128)} %weight_ref.1) | copy-start | bytes 76
